TPU v7x, 256 devices: a whole 4x4x8 slice. The times are simulated.
256 devices in a mesh: orb: 8 (over x, core), dom: 32 (over y, z).
Axes of the slice: x: 4, y: 4, z: 8, core: 2. Of those that a mesh axis runs over, the one named last changes fastest.
Arguments:
- orbitals: float32 [768, 128, 8, 128], P('orb', 'dom'), may hold values from -6 to 6
- potential: float32 [128, 8, 128], P('dom'), may hold values from -1 to 3
- prev_gradient: float32 [768, 128, 8, 128], P('orb', 'dom'), may hold values from -24 to 24
- prev_direction: float32 [768, 128, 8, 128], P('orb', 'dom'), may hold values from -24 to 24
Outputs:
- new_orbitals: float32 [768, 128, 8, 128], P('orb', 'dom')
- new_direction: float32 [768, 128, 8, 128], P('orb', 'dom')
- gradient: float32 [768, 128, 8, 128], P('orb', 'dom')
All inputs are finite; a program needn't handle non-finite values.
Results may differ from a plain program's by a relative error of at most 0.0002.
Values sent between devices are 32-bit elements; how exact they have to be, the bound alone decides.
No kernel may reach another device: no remote copies, remote signals or barrier semaphores. Data moves between devices by JAX's collectives and lax.ppermute only.
A program may use at most 128 MiB of HBM per device.

v0:
```python
import jax
import jax.numpy as jnp
from jax import lax
from jax.sharding import PartitionSpec as P

coeffs = (-205.0 / 72.0, 8.0 / 5.0, -1.0 / 5.0, 8.0 / 315.0, -1.0 / 560.0)
step_length = 0.05


def padded_2(cells, sides, width):
    for axis, dim in sides:
        count = lax.axis_size(axis)
        ends = count - 1
        head = lax.slice_in_dim(cells, 0, width, axis=dim)
        tail = lax.slice_in_dim(cells, cells.shape[dim] - width, cells.shape[dim], axis=dim)
        cells = jnp.concatenate(
            [
                lax.ppermute(tail, axis, [(i, (i + 1) % count) for i in range(ends)]),
                cells,
                lax.ppermute(head, axis, [((i + 1) % count, i) for i in range(ends)]),
            ],
            axis=dim,
        )
    return cells


def laplace(padded, planes, lines, columns):
    center = padded[:, 4 : 4 + planes, 4 : 4 + lines, 4 : 4 + columns]
    total = 3.0 * coeffs[0] * center
    for offset in range(1, 5):
        total = total + coeffs[offset] * (
            padded[:, 4 + offset : 4 + offset + planes, 4 : 4 + lines, 4 : 4 + columns]
            + padded[:, 4 - offset : 4 - offset + planes, 4 : 4 + lines, 4 : 4 + columns]
        )
        total = total + coeffs[offset] * (
            padded[:, 4 : 4 + planes, 4 + offset : 4 + offset + lines, 4 : 4 + columns]
            + padded[:, 4 : 4 + planes, 4 - offset : 4 - offset + lines, 4 : 4 + columns]
        )
        total = total + coeffs[offset] * (
            padded[:, 4 : 4 + planes, 4 : 4 + lines, 4 + offset : 4 + offset + columns]
            + padded[:, 4 : 4 + planes, 4 : 4 + lines, 4 - offset : 4 - offset + columns]
        )
    return total


def highdot(left, right):
    return jnp.dot(left, right, precision=lax.Precision.HIGHEST, preferred_element_type=jnp.float32)


def on_device(orbitals, potential, prev_gradient, prev_direction):
    block = orbitals.shape[0]
    extended = padded_2(orbitals, (("dom", 1),), 4)
    padded = jnp.pad(extended, ((0, 0), (0, 0), (4, 4), (4, 4)))
    lap = laplace(padded, orbitals.shape[1], orbitals.shape[2], orbitals.shape[3])
    image = -0.5 * lap + potential[None] * orbitals
    cmat = orbitals.reshape(block, -1)
    hmat_rows = image.reshape(block, -1)
    cells = cmat.shape[1] * lax.axis_size("dom")
    cell_orbs, cell_images = (
        lax.all_to_all(cmat, "orb", split_axis=1, concat_axis=0, tiled=True),
        lax.all_to_all(hmat_rows, "orb", split_axis=1, concat_axis=0, tiled=True),
    )
    correlation, hamilton = lax.psum(
        (highdot(cell_orbs, cell_orbs.T), highdot(cell_orbs, cell_images.T)), ("orb", "dom")
    )
    correlation = correlation / cells
    hamilton = hamilton / cells
    cell_grad = (
        4.0 * cell_images
        - 2.0 * highdot(correlation.T, cell_images)
        - 2.0 * highdot(hamilton.T, cell_orbs)
    )
    grad = lax.all_to_all(cell_grad, "orb", split_axis=0, concat_axis=1, tiled=True)
    grad = grad.reshape(orbitals.shape)
    both, cross, before = lax.psum(
        (
            jnp.sum(grad * grad),
            jnp.sum(grad * prev_gradient),
            jnp.sum(prev_gradient * prev_gradient),
        ),
        ("orb", "dom"),
    )
    beta = (both - cross) / before
    direction = -grad + beta * prev_direction
    return (orbitals + step_length * direction, direction, grad)


def solution(mesh):
    in_specs = (
        P("orb", "dom", None, None),
        P("dom", None, None),
        P("orb", "dom", None, None),
        P("orb", "dom", None, None),
    )
    out_specs = (
        P("orb", "dom", None, None),
        P("orb", "dom", None, None),
        P("orb", "dom", None, None),
    )
    return jax.shard_map(
        on_device, mesh=mesh, in_specs=in_specs, out_specs=out_specs, check_vma=False
    )
```

profile of v0, /device:TPU:1, one launch (start us, length us, event | category | flops | bytes accessed | tf_op | source)
XLA Modules:
  0.0 553.9 jit_solution(16415115841045701364)
XLA Ops:
  7.2 5.5 collective-permute-start.1
  12.7 1.3 collective-permute-start
  14.0 1.5 all_to_all.44
  15.5 2.1 copy.16
  17.6 5.3 all-to-all-start.1
  22.8 0.0 copy-start
  22.8 22.1 %collective-permute-done.1 = f32[96,4,8,128]{3,2,1,0:T(8,128)} collective-permute-done((f32[96,4,8,128]{3,2,1,0:T(8,128)}, f32[96,4,8,128]{3,2,1,0:T(8,128)}, u32[]{:S(2)}, u32[]{:S(2)}) %collective-permute-start.1) | collective-permute-done | bytes 1572896 | tf_op jit(solution)/shard_map/ppermute | solution.py:18
  44.9 2.7 constant_dynamic-update-slice_fusion.3
  47.6 0.0 copy-done
  47.6 2.1 constant_dynamic-update-slice_fusion.1
  49.8 0.1 collective-permute-done
  49.9 11.4 %select_maximum_fusion = f32[96,12,16,136]{3,2,1,0:T(8,128)} fusion(f32[96,4,8,128]{3,2,1,0:T(8,128)} %collective-permute-done, f32[96,4,8,128]{3,2,1,0:T(8,128)S(1)} %copy-done, f32[96,4,8,128]{3,2,1,0:T(8,128)} %collective-permute-done.1), kind=kLoop, calls=%fused_computation.4 | loop fusion | flops 37601280 | bytes 14745600 | tf_op jit(solution)/shard_map/concatenate | solution.py:16
  61.3 0.0 copy-start.2
  61.3 2.8 constant_dynamic-update-slice_fusion
  64.0 0.0 copy-done.2
  64.0 41.4 %fusion.10 = f32[96,4,8,128]{3,2,1,0:T(8,128)} fusion(f32[96,12,16,136]{3,2,1,0:T(8,128)} %select_maximum_fusion, f32[96,8,8,128]{3,2,1,0:T(8,128)} %get-tuple-element.13, f32[96,8,8,128]{3,2,1,0:T(8,128)} %constant_dynamic-update-slice_fusion, f32[96,4,8,128]{3,2,1,0:T(8,128)S(1)} %copy-done, f32[96,4,8,128]{3,2,1,0:T(8,128)} %collective-permute-done, ...), kind=kLoop, calls=%fused_computation.18 | loop fusion | flops 15728640 | bytes 40910848 | tf_op jit(solution)/shard_map/add | solution.py:55
  105.5 2.6 all_to_all.40
  108.0 3.5 copy.15
  111.5 0.0 all-to-all-done.1
  111.5 6.1 %all-to-all-start = ((f32[96,8,512]{2,0,1:T(8,128)}), f32[96,8,512]{2,0,1:T(8,128)}, u32[]{:S(2)}, u32[]{:S(2)}) async-start(f32[96,8,512]{2,0,1:T(8,128)} %copy.15), calls=%async_computation | async-start | bytes 3145728 | tf_op jit(solution)/shard_map/all_to_all | solution.py:61
  117.6 0.0 all-reduce.5.cloned.1.call-start
  117.6 5.4 fusion.38
  123.0 15.3 %all-to-all-done = f32[96,8,512]{2,0,1:T(8,128)} async-done(((f32[96,8,512]{2,0,1:T(8,128)}), f32[96,8,512]{2,0,1:T(8,128)}, u32[]{:S(2)}, u32[]{:S(2)}) %all-to-all-start) | async-done | bytes 1572896 | tf_op jit(solution)/shard_map/all_to_all | solution.py:61
  138.3 6.8 %convolution_bitcast_fusion = f32[768,768]{1,0:T(8,128)} fusion(f32[768,512]{1,0:T(8,128)} %bitcast.1, f32[768,512]{1,0:T(8,128)S(1)} %bitcast.22), kind=kOutput, calls=%fused_computation.13 | convolution fusion | flops 3623878656 | bytes 5505024 | tf_op jit(solution)/shard_map/dot_general | solution.py:47
  145.1 0.0 all-reduce.5.cloned.1.call-update
  145.1 273.7 %all-reduce.5.cloned.1.call-done = (f32[768,768]{1,0:T(8,128)}, f32[768,768]{1,0:T(8,128)}) async-done(((f32[768,768]{1,0:T(8,128)}, f32[768,768]{1,0:T(8,128)}), (f32[768,768]{1,0:T(8,128)}, f32[768,768]{1,0:T(8,128)})) %all-reduce.5.cloned.1.call-update) | async-done | bytes 4718608 | tf_op jit(solution)/shard_map/psum | solution.py:63
  418.9 0.0 copy-start.1
  418.9 5.7 %fusion.3 = f32[768,512]{1,0:T(8,128)S(1)} fusion(f32[768,512]{1,0:T(8,128)S(1)} %bitcast.23, f32[768,768]{1,0:T(8,128)} %get-tuple-element.8), kind=kOutput, calls=%fused_computation.9 | convolution fusion | flops 3624468480 | bytes 5505024 | tf_op jit(solution)/shard_map/dot_general | solution.py:47
  424.6 0.0 copy-done.1
  424.6 6.3 %multiply_subtract_fusion = f32[768,512]{1,0:T(8,128)S(1)} fusion(f32[768,512]{1,0:T(8,128)S(1)} %fusion.3, f32[768,512]{1,0:T(8,128)} %bitcast.1, f32[768,768]{1,0:T(8,128)S(1)} %copy-done.1), kind=kOutput, calls=%fused_computation.55 | convolution fusion | flops 3626434560 | bytes 7077888 | tf_op jit(solution)/shard_map/dot_general | solution.py:47
  430.9 27.0 %all_to_all.54 = f32[8,96,512]{2,1,0:T(8,128)S(1)} all-to-all(f32[8,96,512]{2,1,0:T(8,128)S(1)} %bitcast.25), channel_id=1, replica_groups=mesh['orb'=8,'dom'=32] {'orb'}, dimensions={0} | all-to-all | bytes 3145728 | tf_op jit(solution)/shard_map/all_to_all | solution.py:73
  457.9 2.1 copy.18
  459.9 2.4 reshape.24
  462.4 2.9 multiply_reduce_fusion
  465.3 1.0 multiply_reduce_fusion.2
  466.3 74.7 %all-reduce.1 = (f32[]{:T(128)}, f32[]{:T(128)}, f32[]{:T(128)}) all-reduce(f32[]{:T(128)} %multiply_reduce_fusion.2, f32[]{:T(128)} %get-tuple-element.4, f32[]{:T(128)} %get-tuple-element.3), channel_id=1, replica_groups=mesh['orb'=8,'dom'=32] {'orb','dom'}, use_global_device_ids=true, to_apply=%region_3.4 | all-reduce | flops 3 | bytes 24 | tf_op jit(solution)/shard_map/psum | solution.py:75
  542.9 4.1 multiply_add_fusion
Async XLA Ops:
  7.2 37.7 %collective-permute-start.1 = (f32[96,4,8,128]{3,2,1,0:T(8,128)}, f32[96,4,8,128]{3,2,1,0:T(8,128)}, u32[]{:S(2)}, u32[]{:S(2)}) collective-permute-start(f32[96,4,8,128]{3,2,1,0:T(8,128)} %param.4), channel_id=1, source_target_pairs={{0,1},{1,2},{2,3},{3,4},{4,5},{5,6},{6,7},{7,8},{8,9},{9,10},{10,1... | collective-permute-start | bytes 4718600 | tf_op jit(solution)/shard_map/ppermute | solution.py:18
  12.7 37.2 %collective-permute-start = (f32[96,4,8,128]{3,2,1,0:T(8,128)}, f32[96,4,8,128]{3,2,1,0:T(8,128)}, u32[]{:S(2)}, u32[]{:S(2)}) collective-permute-start(f32[96,4,8,128]{3,2,1,0:T(8,128)} %param.4), channel_id=1, source_target_pairs={{1,0},{2,1},{3,2},{4,3},{5,4},{6,5},{7,6},{8,7},{9,8},{10,9},{11,1... | collective-permute-start | bytes 4718600 | tf_op jit(solution)/shard_map/ppermute | solution.py:20
  17.6 93.9 %all-to-all-start.1 = ((f32[96,8,512]{2,0,1:T(8,128)}), f32[96,8,512]{2,0,1:T(8,128)S(1)}, u32[]{:S(2)}, u32[]{:S(2)}) async-start(f32[96,8,512]{2,0,1:T(8,128)} %copy.16), calls=%async_computation.1 | async-start | bytes 3145728 | tf_op jit(solution)/shard_map/all_to_all | solution.py:60
  22.8 24.8 %copy-start = (f32[96,4,8,128]{3,2,1,0:T(8,128)S(1)}, f32[96,4,8,128]{3,2,1,0:T(8,128)}, u32[]{:S(2)}) copy-start(f32[96,4,8,128]{3,2,1,0:T(8,128)} %param.4) | copy-start | bytes 4718596
  61.3 2.8 copy-start.2
  111.5 26.8 %all-to-all-start = ((f32[96,8,512]{2,0,1:T(8,128)}), f32[96,8,512]{2,0,1:T(8,128)}, u32[]{:S(2)}, u32[]{:S(2)}) async-start(f32[96,8,512]{2,0,1:T(8,128)} %copy.15), calls=%async_computation | async-start | bytes 3145728 | tf_op jit(solution)/shard_map/all_to_all | solution.py:61
  117.6 301.2 %all-reduce.5.cloned.1.call-start = ((), (), s32[]{:S(2)}) async-start(), calls=%async_computation.3 | async-start | bytes 9437184 | tf_op jit(solution)/shard_map/psum | solution.py:63
  418.9 5.7 %copy-start.1 = (f32[768,768]{1,0:T(8,128)S(1)}, f32[768,768]{1,0:T(8,128)}, u32[]{:S(2)}) copy-start(f32[768,768]{1,0:T(8,128)} %get-tuple-element.9) | copy-start | bytes 7077892
Sparse Core Ops, SparseCore 0:
  145.2 273.5 all-reduce.4
where the time goes:
time: 555 us; the launch traced here: 554 us
  waiting for transfers between devices  311 us (56%)
  blocking collectives  102 us (18%)
  other arithmetic  60.9 us (11%)
  matrix products  24.2 us (4%)
  local copies, waits for them, and re-layouts  21.7 us (4%)
  starting transfers between devices  18.2 us (3%)
  between operations  16 us (3%)
    psum x1, waiting for transfers between devices, on_device(): lax.psum((highdot(cell_orbs, cell_orbs.T), highdot(cell_orbs, cell_images...  274 us
    psum x1, blocking collectives, on_device(): lax.psum((jnp.sum(grad * grad), jnp.sum(grad * prev_gradient), jnp.sum(pr...  74.7 us
    add x1, other arithmetic, on_device(): image = -0.5 * lap + potential[None] * orbitals  41.4 us
    all_to_all x1, blocking collectives, on_device(): lax.all_to_all(cell_grad, 'orb', split_axis=0, concat_axis=1, tiled=True)  27 us
    dot_general x4, matrix products, highdot(): jnp.dot(left, right, precision=lax.Precision.HIGHEST, preferred_element_t...  24.2 us
    ppermute x1, waiting for transfers between devices, padded_2(): lax.ppermute(tail, axis, [(i, (i + 1) % count) for i in range(ends)])  22.1 us
    all_to_all x1, waiting for transfers between devices, on_device(): lax.all_to_all(hmat_rows, 'orb', split_axis=1, concat_axis=0, tiled=True)  15.3 us
    concatenate x1, other arithmetic, padded_2(): jnp.concatenate([lax.ppermute(tail, axis, [(i, (i + 1) % count) for i in...  11.4 us
  transfers between devices with their start and end apart: 5, of which 4 were waited for; matrix products, arithmetic and copies ran while one was open for 13% of the time, Pallas kernels for 0%

commit v1 on v0

--- a/solution.py
+++ b/solution.py
@@ -2,6 +2,7 @@
 import jax.numpy as jnp
 from jax import lax
 from jax.sharding import PartitionSpec as P
+from jax.lax import all_to_all, axis_size
 
 coeffs = (-205.0 / 72.0, 8.0 / 5.0, -1.0 / 5.0, 8.0 / 315.0, -1.0 / 560.0)
 step_length = 0.05
@@ -70,7 +71,11 @@
         - 2.0 * highdot(correlation.T, cell_images)
         - 2.0 * highdot(hamilton.T, cell_orbs)
     )
-    grad = lax.all_to_all(cell_grad, "orb", split_axis=0, concat_axis=1, tiled=True)
+    w1 = axis_size("orb")
+    carry = jnp.split(cell_grad, w1, axis=0)
+    shaped = jnp.stack(carry, axis=0)
+    wide_out = all_to_all(shaped, "orb", 0, 0)
+    grad = jnp.concatenate(wide_out, axis=1)
     grad = grad.reshape(orbitals.shape)
     both, cross, before = lax.psum(
         (

time: 555 us -> 555 us (level)
  no operation moved by 1% of the time
where the time goes in v1:
time: 555 us; the launch traced here: 554 us
  waiting for transfers between devices  311 us (56%)
  blocking collectives  102 us (18%)
  other arithmetic  60.9 us (11%)
  matrix products  24.2 us (4%)
  local copies, waits for them, and re-layouts  21.8 us (4%)
  starting transfers between devices  18.2 us (3%)
  between operations  16.1 us (3%)
    psum x1, waiting for transfers between devices, on_device(): lax.psum((highdot(cell_orbs, cell_orbs.T), highdot(cell_orbs, cell_images...  274 us
    psum x1, blocking collectives, on_device(): lax.psum((jnp.sum(grad * grad), jnp.sum(grad * prev_gradient), jnp.sum(pr...  74.7 us
    add x1, other arithmetic, on_device(): image = -0.5 * lap + potential[None] * orbitals  41.4 us
    all_to_all x1, blocking collectives, on_device(): wide_out = all_to_all(shaped, 'orb', 0, 0)  27 us
    dot_general x4, matrix products, highdot(): jnp.dot(left, right, precision=lax.Precision.HIGHEST, preferred_element_t...  24.2 us
    ppermute x1, waiting for transfers between devices, padded_2(): lax.ppermute(tail, axis, [(i, (i + 1) % count) for i in range(ends)])  22.1 us
    all_to_all x1, waiting for transfers between devices, on_device(): lax.all_to_all(hmat_rows, 'orb', split_axis=1, concat_axis=0, tiled=True)  15.3 us
    concatenate x1, other arithmetic, padded_2(): jnp.concatenate([lax.ppermute(tail, axis, [(i, (i + 1) % count) for i in...  11.4 us
  transfers between devices with their start and end apart: 5, of which 4 were waited for; matrix products, arithmetic and copies ran while one was open for 13% of the time, Pallas kernels for 0%

profile of v1, /device:TPU:1, one launch (start us, length us, event | category | flops | bytes accessed | tf_op | source)
XLA Modules:
  0.0 554.1 jit_solution(9070393580727904230)
XLA Ops:
  7.2 5.5 collective-permute-start.1
  12.7 1.3 collective-permute-start
  14.0 1.5 all_to_all.35
  15.5 2.1 copy.15
  17.6 5.3 all-to-all-start.1
  22.8 0.0 copy-start
  22.8 22.1 %collective-permute-done.1 = f32[96,4,8,128]{3,2,1,0:T(8,128)} collective-permute-done((f32[96,4,8,128]{3,2,1,0:T(8,128)}, f32[96,4,8,128]{3,2,1,0:T(8,128)}, u32[]{:S(2)}, u32[]{:S(2)}) %collective-permute-start.1) | collective-permute-done | bytes 1572896 | tf_op jit(solution)/shard_map/ppermute | solution.py:19
  44.9 2.7 constant_dynamic-update-slice_fusion.3
  47.6 0.0 copy-done
  47.6 2.1 constant_dynamic-update-slice_fusion.1
  49.8 0.1 collective-permute-done
  49.9 11.4 %select_maximum_fusion = f32[96,12,16,136]{3,2,1,0:T(8,128)} fusion(f32[96,4,8,128]{3,2,1,0:T(8,128)} %collective-permute-done, f32[96,4,8,128]{3,2,1,0:T(8,128)S(1)} %copy-done, f32[96,4,8,128]{3,2,1,0:T(8,128)} %collective-permute-done.1), kind=kLoop, calls=%fused_computation.4 | loop fusion | flops 37601280 | bytes 14745600 | tf_op jit(solution)/shard_map/concatenate | solution.py:17
  61.3 0.0 copy-start.2
  61.3 2.8 constant_dynamic-update-slice_fusion
  64.0 0.0 copy-done.2
  64.0 41.4 %fusion.10 = f32[96,4,8,128]{3,2,1,0:T(8,128)} fusion(f32[96,12,16,136]{3,2,1,0:T(8,128)} %select_maximum_fusion, f32[96,8,8,128]{3,2,1,0:T(8,128)} %get-tuple-element.13, f32[96,8,8,128]{3,2,1,0:T(8,128)} %constant_dynamic-update-slice_fusion, f32[96,4,8,128]{3,2,1,0:T(8,128)S(1)} %copy-done, f32[96,4,8,128]{3,2,1,0:T(8,128)} %collective-permute-done, ...), kind=kLoop, calls=%fused_computation.18 | loop fusion | flops 15728640 | bytes 40910848 | tf_op jit(solution)/shard_map/add | solution.py:56
  105.5 2.6 all_to_all.31
  108.0 3.5 copy.14
  111.5 0.0 all-to-all-done.1
  111.5 6.1 %all-to-all-start = ((f32[96,8,512]{2,0,1:T(8,128)}), f32[96,8,512]{2,0,1:T(8,128)}, u32[]{:S(2)}, u32[]{:S(2)}) async-start(f32[96,8,512]{2,0,1:T(8,128)} %copy.14), calls=%async_computation | async-start | bytes 3145728 | tf_op jit(solution)/shard_map/all_to_all | solution.py:62
  117.6 0.0 all-reduce.5.cloned.1.call-start
  117.6 5.4 fusion.46
  123.0 15.3 %all-to-all-done = f32[96,8,512]{2,0,1:T(8,128)} async-done(((f32[96,8,512]{2,0,1:T(8,128)}), f32[96,8,512]{2,0,1:T(8,128)}, u32[]{:S(2)}, u32[]{:S(2)}) %all-to-all-start) | async-done | bytes 1572896 | tf_op jit(solution)/shard_map/all_to_all | solution.py:62
  138.3 6.8 %convolution_bitcast_fusion = f32[768,768]{1,0:T(8,128)} fusion(f32[768,512]{1,0:T(8,128)} %bitcast.1, f32[768,512]{1,0:T(8,128)S(1)} %bitcast.53), kind=kOutput, calls=%fused_computation.13 | convolution fusion | flops 3623878656 | bytes 5505024 | tf_op jit(solution)/shard_map/dot_general | solution.py:48
  145.1 0.0 all-reduce.5.cloned.1.call-update
  145.1 273.7 %all-reduce.5.cloned.1.call-done = (f32[768,768]{1,0:T(8,128)}, f32[768,768]{1,0:T(8,128)}) async-done(((f32[768,768]{1,0:T(8,128)}, f32[768,768]{1,0:T(8,128)}), (f32[768,768]{1,0:T(8,128)}, f32[768,768]{1,0:T(8,128)})) %all-reduce.5.cloned.1.call-update) | async-done | bytes 4718608 | tf_op jit(solution)/shard_map/psum | solution.py:64
  418.9 0.0 copy-start.1
  418.9 5.7 %fusion.3 = f32[768,512]{1,0:T(8,128)S(1)} fusion(f32[768,512]{1,0:T(8,128)S(1)} %bitcast.54, f32[768,768]{1,0:T(8,128)} %get-tuple-element.8), kind=kOutput, calls=%fused_computation.9 | convolution fusion | flops 3624468480 | bytes 5505024 | tf_op jit(solution)/shard_map/dot_general | solution.py:48
  424.6 0.0 copy-done.1
  424.6 6.3 %multiply_subtract_fusion = f32[768,512]{1,0:T(8,128)S(1)} fusion(f32[768,512]{1,0:T(8,128)S(1)} %fusion.3, f32[768,512]{1,0:T(8,128)} %bitcast.1, f32[768,768]{1,0:T(8,128)S(1)} %copy-done.1), kind=kOutput, calls=%fused_computation.55 | convolution fusion | flops 3626434560 | bytes 7077888 | tf_op jit(solution)/shard_map/dot_general | solution.py:48
  431.1 27.0 %all_to_all.43 = f32[8,96,512]{2,1,0:T(8,128)S(1)} all-to-all(f32[8,96,512]{2,1,0:T(8,128)S(1)} %fusion.36), channel_id=1, replica_groups=mesh['orb'=8,'dom'=32] {'orb'}, dimensions={0} | all-to-all | bytes 3145728 | tf_op jit(solution)/shard_map/all_to_all | solution.py:77
  458.0 2.1 copy.17
  460.1 2.4 reshape_reshape.3
  462.5 2.9 multiply_reduce_fusion
  465.5 1.0 multiply_reduce_fusion.2
  466.5 74.7 %all-reduce.1 = (f32[]{:T(128)}, f32[]{:T(128)}, f32[]{:T(128)}) all-reduce(f32[]{:T(128)} %multiply_reduce_fusion.2, f32[]{:T(128)} %get-tuple-element.4, f32[]{:T(128)} %get-tuple-element.3), channel_id=1, replica_groups=mesh['orb'=8,'dom'=32] {'orb','dom'}, use_global_device_ids=true, to_apply=%region_3.4 | all-reduce | flops 3 | bytes 24 | tf_op jit(solution)/shard_map/psum | solution.py:80
  543.1 4.1 multiply_add_fusion
  (8 shorter events, 0.1 us)
Async XLA Ops:
  7.2 37.7 %collective-permute-start.1 = (f32[96,4,8,128]{3,2,1,0:T(8,128)}, f32[96,4,8,128]{3,2,1,0:T(8,128)}, u32[]{:S(2)}, u32[]{:S(2)}) collective-permute-start(f32[96,4,8,128]{3,2,1,0:T(8,128)} %param.4), channel_id=1, source_target_pairs={{0,1},{1,2},{2,3},{3,4},{4,5},{5,6},{6,7},{7,8},{8,9},{9,10},{10,1... | collective-permute-start | bytes 4718600 | tf_op jit(solution)/shard_map/ppermute | solution.py:19
  12.7 37.2 %collective-permute-start = (f32[96,4,8,128]{3,2,1,0:T(8,128)}, f32[96,4,8,128]{3,2,1,0:T(8,128)}, u32[]{:S(2)}, u32[]{:S(2)}) collective-permute-start(f32[96,4,8,128]{3,2,1,0:T(8,128)} %param.4), channel_id=1, source_target_pairs={{1,0},{2,1},{3,2},{4,3},{5,4},{6,5},{7,6},{8,7},{9,8},{10,9},{11,1... | collective-permute-start | bytes 4718600 | tf_op jit(solution)/shard_map/ppermute | solution.py:21
  17.6 93.9 %all-to-all-start.1 = ((f32[96,8,512]{2,0,1:T(8,128)}), f32[96,8,512]{2,0,1:T(8,128)S(1)}, u32[]{:S(2)}, u32[]{:S(2)}) async-start(f32[96,8,512]{2,0,1:T(8,128)} %copy.15), calls=%async_computation.1 | async-start | bytes 3145728 | tf_op jit(solution)/shard_map/all_to_all | solution.py:61
  22.8 24.8 %copy-start = (f32[96,4,8,128]{3,2,1,0:T(8,128)S(1)}, f32[96,4,8,128]{3,2,1,0:T(8,128)}, u32[]{:S(2)}) copy-start(f32[96,4,8,128]{3,2,1,0:T(8,128)} %param.4) | copy-start | bytes 4718596
  61.3 2.8 copy-start.2
  111.5 26.8 %all-to-all-start = ((f32[96,8,512]{2,0,1:T(8,128)}), f32[96,8,512]{2,0,1:T(8,128)}, u32[]{:S(2)}, u32[]{:S(2)}) async-start(f32[96,8,512]{2,0,1:T(8,128)} %copy.14), calls=%async_computation | async-start | bytes 3145728 | tf_op jit(solution)/shard_map/all_to_all | solution.py:62
  117.6 301.2 %all-reduce.5.cloned.1.call-start = ((), (), s32[]{:S(2)}) async-start(), calls=%async_computation.3 | async-start | bytes 9437184 | tf_op jit(solution)/shard_map/psum | solution.py:64
  418.9 5.7 %copy-start.1 = (f32[768,768]{1,0:T(8,128)S(1)}, f32[768,768]{1,0:T(8,128)}, u32[]{:S(2)}) copy-start(f32[768,768]{1,0:T(8,128)} %get-tuple-element.9) | copy-start | bytes 7077892
Sparse Core Ops, SparseCore 0:
  145.2 273.5 all-reduce.4
